TPU v7x, 32 devices: a whole 2x2x4 slice. The times are simulated.
32 devices in a mesh: seq: 8 (over z, x), fsdp: 4 (over y, core).
Axes of the slice: x: 2, y: 2, z: 4, core: 2. Of those that a mesh axis runs over, the one named last changes fastest.
Arguments:
- tokens: bfloat16 [4, 2048, 1536], P('fsdp', 'seq'), may hold values from -6 to 6
- lengths: int32 [4], P('fsdp'), may hold values from 512 to 2048, as said below
- norm_gain: bfloat16 [1536], P('fsdp'), may hold values from 0.099609375 to 1.8984375
- in_weight: bfloat16 [1536, 6448], P('fsdp'), may hold values from -0.15625 to 0.15625
- conv_weight: bfloat16 [4, 3328], P(None, 'fsdp'), may hold values from -3 to 3
- conv_bias: bfloat16 [3328], P('fsdp'), may hold values from -0.5 to 0.5
- dt_bias: bfloat16 [48], P('fsdp'), may hold values from -4.5 to -3.5
- decay_log: bfloat16 [48], P('fsdp'), may hold values from -9 to 0
- skip_gain: bfloat16 [48], P('fsdp'), may hold values from 0.5 to 1.5
- gated_gain: bfloat16 [3072], P('fsdp'), may hold values from 0.099609375 to 1.8984375
- out_weight: bfloat16 [3072, 1536], P('fsdp'), may hold values from -0.109375 to 0.109375
- cotangent: bfloat16 [4, 2048, 1536], P('fsdp', 'seq'), may hold values from -6 to 6
Outputs:
- mixed: bfloat16 [4, 2048, 1536], P('fsdp', 'seq')
- input_grad: float32 [4, 2048, 1536], P('fsdp', 'seq')
- norm_gain_grad: float32 [1536], P('fsdp')
- in_weight_grad: float32 [1536, 6448], P('fsdp')
- conv_weight_grad: float32 [4, 3328], P(None, 'fsdp')
- conv_bias_grad: float32 [3328], P('fsdp')
- dt_bias_grad: float32 [48], P('fsdp')
- decay_log_grad: float32 [48], P('fsdp')
- skip_gain_grad: float32 [48], P('fsdp')
- gated_gain_grad: float32 [3072], P('fsdp')
- out_weight_grad: float32 [3072, 1536], P('fsdp')
Inputs may be any that keep to these rules, and one draw needn't show every extreme that they name: `lengths`: each slot's valid positions come first; some slot has all 2048 valid.
All inputs are finite; a program needn't handle non-finite values.
Results may differ from a plain program's by a relative error of at most 0.012.
The roundings to bfloat16 on the way count: a program that leaves them out, or rounds other values in their place, can miss the bound.
Values may be sent and summed in bfloat16 or wider, within the bound.
No kernel may reach another device: no remote copies, remote signals or barrier semaphores. Data moves between devices by JAX's collectives and lax.ppermute only.
A program may use at most 256 MiB of HBM per device.

v0:
```python
import jax
import jax.numpy as jnp
from jax import lax
from jax.sharding import PartitionSpec as P

epsilon = 1e-05
triple = lax.Precision.HIGH


def from_behind(value, axis, by):
    count = lax.axis_size(axis)
    pairs = [(i, i + by) for i in range(count) if 0 <= i + by < count]
    return lax.ppermute(value, axis, pairs)


def carried_in(value, axis, combine, identity, reverse):
    count, position = (lax.axis_size(axis), lax.axis_index(axis))
    everything = jax.tree.map(lambda part: lax.all_gather(part, axis), value)
    start = jax.tree.map(
        lambda part, zero: jnp.broadcast_to(jnp.asarray(zero, part.dtype), part.shape),
        value,
        identity,
    )

    def lap(k, before):
        at = count - 1 - k if reverse else k
        reached = at > position if reverse else at < position
        new = combine(before, jax.tree.map(lambda part: part[at], everything))
        return jax.tree.map(lambda a, b: jnp.where(reached, a, b), new, before)

    return lax.fori_loop(0, count, lap, start)


def rms_scale(inputs, gain):
    inv_rms = lax.rsqrt(jnp.mean(inputs * inputs, axis=-1, keepdims=True) + epsilon)
    return inputs * inv_rms * gain


def convolve(extended, conv_w, conv_b):
    taps = conv_w.shape[0]
    count = extended.shape[1] - taps + 1
    summed = conv_b + jnp.zeros(extended[:, :count].shape, jnp.float32)
    for offset in range(taps):
        summed = summed + extended[:, offset : offset + count] * conv_w[offset]
    return jax.nn.silu(summed)


def local_scan(values, b_rows, c_rows, step_raw, dt_b, decay_l):
    step_size = jax.nn.softplus(step_raw + dt_b)
    log_decay = jnp.cumsum(-step_size * jnp.exp(decay_l), axis=1)
    count = values.shape[1]
    places = jnp.arange(count)
    lower = (places[:, None] >= places[None, :])[None, :, :, None]
    gaps = log_decay[:, :, None, :] - log_decay[:, None, :, :]
    weights = jnp.where(lower, jnp.exp(jnp.where(lower, gaps, 0.0)), 0.0)
    intersection = jnp.einsum("stn,sun->stu", c_rows, b_rows, precision=triple)
    mixing = weights * intersection[..., None] * step_size[:, None, :, :]
    local_out = jnp.einsum("stuh,suhp->sthp", mixing, values, precision=triple)
    to_end = jnp.exp(log_decay[:, -1:, :] - log_decay) * step_size
    local_state = jnp.einsum("sqh,sqhp,sqn->shpn", to_end, values, b_rows, precision=triple)
    return (local_out, local_state, jnp.exp(log_decay[:, -1, :]), jnp.exp(log_decay))


def finish(local_out, c_rows, decay_in, state_in, values, skip_g, gate_part, gated_g):
    carried_out = decay_in[..., None] * jnp.einsum(
        "sqn,shpn->sqhp", c_rows, state_in, precision=triple
    )
    mixed_heads = local_out + carried_out + skip_g[:, None] * values
    flat = mixed_heads.reshape(gate_part.shape)
    return rms_scale(flat * jax.nn.silu(gate_part), gated_g)


def chain(earlier, later):
    return (earlier[0] * later[0], later[0][..., None, None] * earlier[1] + later[1])


def per_device(
    tokens,
    lengths,
    norm_gain,
    in_weight,
    conv_weight,
    conv_bias,
    dt_bias,
    decay_log,
    skip_gain,
    gated_gain,
    out_weight,
    cotangent,
):
    gathered = (
        lax.all_gather(norm_gain, "fsdp", axis=0, tiled=True),
        lax.all_gather(in_weight, "fsdp", axis=0, tiled=True),
        lax.all_gather(conv_weight, "fsdp", axis=1, tiled=True),
        lax.all_gather(conv_bias, "fsdp", axis=0, tiled=True),
        lax.all_gather(dt_bias, "fsdp", axis=0, tiled=True),
        lax.all_gather(decay_log, "fsdp", axis=0, tiled=True),
        lax.all_gather(skip_gain, "fsdp", axis=0, tiled=True),
        lax.all_gather(gated_gain, "fsdp", axis=0, tiled=True),
        lax.all_gather(out_weight, "fsdp", axis=0, tiled=True),
    )
    full_in = gathered[1]
    full_out = gathered[8]
    norm_f, conv_wf, conv_bf, dtb_f, decay_f, skip_f, ggain_f = [
        gathered[index].astype(jnp.float32) for index in (0, 2, 3, 4, 5, 6, 7)
    ]
    slots, seg, width = tokens.shape
    inner = full_out.shape[0]
    heads = dtb_f.shape[0]
    head_size = inner // heads
    conv_width = conv_wf.shape[1]
    state_width = (conv_width - inner) // 2
    taps = conv_wf.shape[0]
    places = lax.axis_index("seq") * seg + jnp.arange(seg)
    valid = (places[None, :] < lengths[:, None]).astype(jnp.float32)
    inputs = tokens.astype(jnp.float32)
    normed_f, pull_norm = jax.vjp(rms_scale, inputs, norm_f)
    normed = normed_f.astype(jnp.bfloat16)
    projected = jnp.einsum(
        "sqd,dp->sqp", normed, full_in, preferred_element_type=jnp.float32
    ).astype(jnp.bfloat16)
    gate_part = projected[..., :inner].astype(jnp.float32)
    conv_in = projected[..., inner : inner + conv_width]
    step_raw = projected[..., inner + conv_width :].astype(jnp.float32)
    previous = from_behind(conv_in[:, seg - (taps - 1) :], "seq", 1)
    extended = jnp.concatenate([previous, conv_in], axis=1).astype(jnp.float32)
    activated_f, pull_conv = jax.vjp(convolve, extended, conv_wf, conv_bf)
    activated = lax.optimization_barrier(activated_f.astype(jnp.bfloat16)).astype(jnp.float32)
    values = activated[..., :inner].reshape(slots, seg, heads, head_size)
    b_rows = activated[..., inner : inner + state_width]
    c_rows = activated[..., inner + state_width :]
    scanned, pull_local = jax.vjp(local_scan, values, b_rows, c_rows, step_raw, dtb_f, decay_f)
    local_out, local_state, whole_decay, decay_in = scanned
    identity = (
        jnp.ones((slots, heads), jnp.float32),
        jnp.zeros((slots, heads, head_size, state_width), jnp.float32),
    )
    state_in = carried_in((whole_decay, local_state), "seq", chain, identity, False)[1]
    gated_f, pull_finish = jax.vjp(
        finish, local_out, c_rows, decay_in, state_in, values, skip_f, gate_part, ggain_f
    )
    gated_out = gated_f.astype(jnp.bfloat16)
    branch = jnp.einsum("sqi,id->sqd", gated_out, full_out, preferred_element_type=jnp.float32)
    mixed = (valid[..., None] * (inputs + branch)).astype(jnp.bfloat16)
    back_in, back_out = (
        lax.all_gather(in_weight, "fsdp", axis=0, tiled=True),
        lax.all_gather(out_weight, "fsdp", axis=0, tiled=True),
    )
    upstream = valid[..., None] * cotangent.astype(jnp.float32)
    back_branch = upstream.astype(jnp.bfloat16)
    grad_out_w = jnp.einsum(
        "sqi,sqd->id", gated_out, back_branch, preferred_element_type=jnp.float32
    )
    back_gated = jnp.einsum(
        "sqd,id->sqi", back_branch, back_out, preferred_element_type=jnp.float32
    )
    d_local, d_crows_one, d_decay_in, d_state_local, d_values_one, d_skip, d_gate, d_ggain = (
        pull_finish(back_gated)
    )
    state_after = carried_in((whole_decay, d_state_local), "seq", chain, identity, True)[1]
    d_whole = jnp.sum(state_after * state_in, axis=(2, 3))
    d_values_two, d_brows, d_crows_two, d_step, d_dtb, d_decay = pull_local(
        (d_local, state_after, d_whole, d_decay_in)
    )
    d_active = jnp.concatenate(
        [
            (d_values_one + d_values_two).reshape(slots, seg, inner),
            d_brows,
            d_crows_one + d_crows_two,
        ],
        axis=-1,
    )
    d_extended, d_conv_w, d_conv_b = pull_conv(d_active)
    returned = from_behind(d_extended[:, : taps - 1].astype(jnp.bfloat16), "seq", -1).astype(
        jnp.float32
    )
    d_conv_in = d_extended[:, taps - 1 :] + jnp.pad(returned, ((0, 0), (seg - taps + 1, 0), (0, 0)))
    back_projected = jnp.concatenate([d_gate, d_conv_in, d_step], axis=-1).astype(jnp.bfloat16)
    grad_in_w = jnp.einsum(
        "sqd,sqp->dp", normed, back_projected, preferred_element_type=jnp.float32
    )
    back_normed = jnp.einsum(
        "sqp,dp->sqd", back_projected, back_in, preferred_element_type=jnp.float32
    )
    d_inputs, d_norm = pull_norm(back_normed)
    input_grad = upstream + d_inputs
    shares = (
        lax.psum_scatter(d_norm, "fsdp", scatter_dimension=0, tiled=True),
        lax.psum_scatter(grad_in_w, "fsdp", scatter_dimension=0, tiled=True),
        lax.psum_scatter(d_conv_w, "fsdp", scatter_dimension=1, tiled=True),
        lax.psum_scatter(d_conv_b, "fsdp", scatter_dimension=0, tiled=True),
        lax.psum_scatter(d_dtb, "fsdp", scatter_dimension=0, tiled=True),
        lax.psum_scatter(d_decay, "fsdp", scatter_dimension=0, tiled=True),
        lax.psum_scatter(d_skip, "fsdp", scatter_dimension=0, tiled=True),
        lax.psum_scatter(d_ggain, "fsdp", scatter_dimension=0, tiled=True),
        lax.psum_scatter(grad_out_w, "fsdp", scatter_dimension=0, tiled=True),
    )
    totals = lax.psum(
        (
            shares[0],
            shares[1],
            shares[2],
            shares[3],
            shares[4],
            shares[5],
            shares[6],
            shares[7],
            shares[8],
        ),
        "seq",
    )
    return (
        mixed,
        input_grad,
        totals[0],
        totals[1],
        totals[2],
        totals[3],
        totals[4],
        totals[5],
        totals[6],
        totals[7],
        totals[8],
    )


def solution(mesh):
    placed = (
        P("fsdp", "seq", None),
        P("fsdp"),
        P("fsdp"),
        P("fsdp", None),
        P(None, "fsdp"),
        P("fsdp"),
        P("fsdp"),
        P("fsdp"),
        P("fsdp"),
        P("fsdp"),
        P("fsdp", None),
        P("fsdp", "seq", None),
    )
    return jax.shard_map(
        per_device,
        mesh=mesh,
        in_specs=placed,
        out_specs=(
            P("fsdp", "seq", None),
            P("fsdp", "seq", None),
            P("fsdp"),
            P("fsdp", None),
            P(None, "fsdp"),
            P("fsdp"),
            P("fsdp"),
            P("fsdp"),
            P("fsdp"),
            P("fsdp"),
            P("fsdp", None),
        ),
        check_vma=False,
    )
```

profile of v0, /device:TPU:0, one launch (start us, length us, event | category | flops | bytes accessed | tf_op | source)
XLA Modules:
  0.0 1545.1 jit_solution(13398759697782761256)
XLA Ops:
  8.1 6.2 all-gather.3
  14.4 5.4 all-gather.2
  22.8 7.5 all-reduce.24
  32.0 105.5 %all-gather.10.cloned.1.call-done = bf16[1536,6448]{0,1:T(8,128)(2,1)} async-done(((bf16[384,6448]{0,1:T(8,128)(2,1)}), bf16[1536,6448]{0,1:T(8,128)(2,1)}) %all-gather.10.cloned.1.call-update) | async-done | bytes 19808272 | tf_op jit(solution)/shard_map/all_gather | solution.py:93
  137.4 9.9 fusion.6
  151.5 4.0 collective-permute-start
  161.4 4.2 multiply_convert_fusion
  170.8 3.6 fusion.22
  176.4 5.2 all-gather.4
  193.9 19.2 %all_gather.53 = f32[8,1,48]{2,1,0:T(1,128)} all-gather(f32[1,1,48]{2,1,0:T(1,128)} %get-tuple-element.423), channel_id=1, replica_groups=mesh['seq'=8,'fsdp'=4] {'seq'}, dimensions={0}, use_global_device_ids=true | all-gather | bytes 1728 | tf_op jit(solution)/shard_map/all_gather | solution.py:18
  213.1 3.6 copy.176
  218.5 131.1 %all-gather.14.cloned.1.call-done = f32[384,64,128]{2,1,0:T(8,128)} async-done(((f32[48,64,128]{2,1,0:T(8,128)}), f32[384,64,128]{2,1,0:T(8,128)}) %all-gather.14.cloned.1.call-update) | async-done | bytes 12582928 | tf_op jit(solution)/shard_map/all_gather | solution.py:18
  349.6 36.0 %while.30 = (s32[]{:T(128)}, f32[1,48,64,128]{3,2,1,0:T(8,128)}, s32[]{:T(128)}, f32[8,1,48]{2,1,0:T(1,128)}, f32[8,1,48,64,128]{4,3,2,1,0:T(8,128)}, /*index=5*/s32[]{:T(128)}, s32[]{:T(128)}) while((s32[]{:T(128)}, f32[1,48,64,128]{3,2,1,0:T(8,128)}, s32[]{:T(128)}, f32[8,1,48]{2,1,0:T(1,128)}, f32[8,1,48,64,128]{4,3,2,1,0:T(8,128)}, ...), condition=%wide.region_4.5_spmd.clone, body=%wide.region_3.4_spmd.clone.sunk | while | flops 1572868 | bytes 4719281 | solution.py:31
  354.7 3.7 fusion.142
  359.5 4.0 fusion.142
  388.6 9.6 fusion.34
  401.8 5.1 multiply_reduce_fusion.7
  408.0 5.7 all-gather.12.cloned.1.call-done
  413.7 10.0 fusion.35
  423.7 5.9 multiply_reduce_fusion.5
  436.8 4.0 fusion.94
  440.9 12.7 fusion.76
  454.0 3.7 copy.179
  457.7 14.9 fusion.8
  474.1 4.2 multiply_reduce_fusion.6
  484.9 5.0 fusion.63
  491.7 125.8 %all-gather.16.cloned.1.call-done = f32[384,64,128]{2,1,0:T(8,128)} async-done(((f32[48,64,128]{2,1,0:T(8,128)}), f32[384,64,128]{2,1,0:T(8,128)}) %all-gather.16.cloned.1.call-update) | async-done | bytes 12582928 | tf_op jit(solution)/shard_map/all_gather | solution.py:18
  617.5 38.9 %while.31 = (s32[]{:T(128)}, f32[1,48,64,128]{3,2,1,0:T(8,128)}, s32[]{:T(128)}, f32[8,1,48]{2,1,0:T(1,128)}, f32[8,1,48,64,128]{4,3,2,1,0:T(8,128)}, /*index=5*/s32[]{:T(128)}, s32[]{:T(128)}, s32[]{:T(128)}, s32[]{:T(128)}) while((s32[]{:T(128)}, f32[1,48,64,128]{3,2,1,0:T(8,128)}, s32[]{:T(128)}, f32[8,1,48]{2,1,0:T(1,128)}, ...), condition=%wide.region_8.9_spmd.clone, body=%wide.region_7.8_spmd.clone.sunk | while | flops 1572872 | bytes 4719343 | solution.py:31
  622.6 4.0 fusion.143
  627.7 4.1 fusion.143
  633.0 4.1 fusion.143
  638.2 4.1 fusion.143
  652.5 3.8 fusion.143
  656.3 5.2 fusion.26
  669.9 3.8 reduce-window.16
  676.4 11.2 fusion.33
  687.6 3.9 copy.190
  691.5 4.7 fusion.69
  696.2 5.5 multiply_reduce_fusion.4
  712.6 18.4 %fusion.61 = f32[1536,6448]{0,1:T(8,128)} fusion(bf16[256,48]{1,0:T(8,128)(2,1)} %bitcast.336, bf16[256,3328]{1,0:T(8,128)(2,1)} %fusion.42, bf16[256,3072]{1,0:T(8,128)(2,1)} %get-tuple-element.412, bf16[1,256,1536]{2,1,0:T(8,128)(2,1)} %param.16, f32[1536]{0:T(1024)S(1)} %reshape.620, f32[256]{0:T(256)S(1)} %fusion.111), kind=kOutput, calls=%fused_computation.114 | convolution fusion | flops 5082390528 | bytes 43711488 | tf_op jit(solution)/shard_map/sqd,sqp->dp/dot_general | solution.py:179
  733.8 23.9 %reduce-scatter.8.cloned.1.call-done = f32[768,1536]{1,0:T(8,128)} async-done(((f32[3072,1536]{1,0:T(8,128)}), f32[768,1536]{1,0:T(8,128)}) %reduce-scatter.8.cloned.1.call-update) | async-done | bytes 4718608 | tf_op jit(solution)/shard_map/reduce_scatter | solution.py:196
  757.6 279.1 %reduce-scatter.6.cloned.1.call-done = f32[384,6448]{0,1:T(8,128)} async-done(((f32[1536,6448]{0,1:T(8,128)}), f32[384,6448]{0,1:T(8,128)}) %reduce-scatter.6.cloned.1.call-update) | async-done | bytes 9904144 | tf_op jit(solution)/shard_map/reduce_scatter | solution.py:189
  1040.0 7.5 fusion.39
  1047.6 10.0 fusion.44
  1057.6 12.3 all-reduce.23
  1073.3 39.6 %all-reduce.21 = (f32[384]{0:T(512)}, f32[4,832]{1,0:T(4,128)}, f32[832]{0:T(1024)}, f32[12]{0:T(128)}, f32[12]{0:T(128)}, /*index=5*/f32[12]{0:T(128)}, f32[768]{0:T(1024)}) all-reduce(f32[384]{0:T(512)S(1)} %dynamic-slice.5, f32[4,832]{1,0:T(4,128)S(1)} %copy.211, ...), channel_id=1, replica_groups=mesh['seq'=8,'fsdp'=4] {'seq'}, use_global_device_ids=true, to_apply=%region_21.22 | all-reduce | flops 5348 | bytes 42784 | tf_op jit(solution)/shard_map/psum | solution.py:198
  1112.9 414.5 %all-reduce.27.cloned.1.call-done = (f32[384,6448]{0,1:T(8,128)}, f32[768,1536]{1,0:T(8,128)}) async-done(((f32[384,6448]{0,1:T(8,128)}, f32[768,1536]{1,0:T(8,128)}), (f32[384,6448]{0,1:T(8,128)}, f32[768,1536]{1,0:T(8,128)})) %all-reduce.27.cloned.1.call-update) | async-done | bytes 14622736 | tf_op jit(solution)/shard_map/psum | solution.py:198
  1527.4 8.5 copy.231
  (270 shorter events, 137.2 us)
Async XLA Ops:
  7.2 12.7 copy-start.52
  7.2 7.2 copy-start.57
  7.2 14.6 copy-start.59
  7.2 14.8 copy-start.60
  7.2 15.1 copy-start.61
  7.2 15.3 copy-start.53
  7.3 24.4 %copy-start.11 = (bf16[1,256,1536]{2,1,0:T(8,128)(2,1)S(1)}, bf16[1,256,1536]{2,1,0:T(8,128)(2,1)}, u32[]{:S(2)}) copy-start(bf16[1,256,1536]{2,1,0:T(8,128)(2,1)} %param.16) | copy-start | bytes 2359300
  7.3 130.2 %all-gather.10.cloned.1.call-start = ((), (), s32[]{:S(2)}) async-start(), calls=%async_computation.3 | async-start | bytes 24760320 | tf_op jit(solution)/shard_map/all_gather | solution.py:93
  8.0 341.6 %all-gather.14.cloned.1.call-start = ((), (), s32[]{:S(2)}) async-start(), calls=%async_computation.7 | async-start | bytes 14155776 | tf_op jit(solution)/shard_map/all_gather | solution.py:18
  30.3 117.0 %copy-start.62 = (bf16[48]{0:T(256)(128)(2,1)}, bf16[48]{0:T(256)(128)(2,1)S(1)}, u32[]{:S(2)}) copy-start(bf16[48]{0:T(256)(128)(2,1)S(1)} %get-tuple-element.398) | copy-start | bytes 292
  30.9 125.8 %copy-start.40 = (f32[48]{0:T(128)}, f32[48]{0:T(128)S(1)}, u32[]{:S(2)}) copy-start(f32[48]{0:T(128)S(1)} %convert_element_type.95) | copy-start | bytes 580
  31.9 115.4 %copy-start.44 = (f32[256]{0:T(256)}, f32[256]{0:T(256)S(1)}, u32[]{:S(2)}) copy-start(f32[256]{0:T(256)S(1)} %fusion.46) | copy-start | bytes 3076
  31.9 115.4 %copy-start.55 = (f32[48]{0:T(128)}, f32[48]{0:T(128)S(1)}, u32[]{:S(2)}) copy-start(f32[48]{0:T(128)S(1)} %convert_exponential_fusion) | copy-start | bytes 580
  147.3 12.2 copy-start.10
  151.5 8.1 collective-permute-start
  170.8 5.6 copy-start.54
  174.5 239.2 %all-gather.12.cloned.1.call-start = ((), (), s32[]{:S(2)}) async-start(), calls=%async_computation.4 | async-start | bytes 11796480 | tf_op jit(solution)/shard_map/all_gather | solution.py:100
  175.2 442.3 %all-gather.16.cloned.1.call-start = ((), (), s32[]{:S(2)}) async-start(), calls=%async_computation.8 | async-start | bytes 14155776 | tf_op jit(solution)/shard_map/all_gather | solution.py:18
  388.2 10.0 copy-start.8
  413.6 10.0 copy-start.47
  413.6 10.0 copy-start
  413.6 10.0 copy-start.3
  413.6 10.0 copy-start.6
  413.6 10.1 copy-start.38
  423.7 7.6 copy-start.9
  440.9 316.7 %reduce-scatter.8.cloned.1.call-start = ((), (), s32[]{:S(2)}) async-start(), calls=%async_computation.6 | async-start | bytes 23592960 | tf_op jit(solution)/shard_map/reduce_scatter | solution.py:196
  453.7 583.1 %reduce-scatter.6.cloned.1.call-start = ((), (), s32[]{:S(2)}) async-start(), calls=%async_computation.5 | async-start | bytes 49520640 | tf_op jit(solution)/shard_map/reduce_scatter | solution.py:189
  483.0 7.0 copy-start.22
  691.5 4.7 copy-start.7
  696.1 5.5 copy-start.29
  696.2 5.5 copy-start.30
  696.2 5.5 copy-start.31
  704.4 6.0 collective-permute-start.1
  731.1 341.0 %reduce-scatter.10.cloned.1.call-start = ((), (), s32[]{:S(2)}) async-start(), calls=%async_computation.9 | async-start | bytes 2129920
  733.7 793.7 %all-reduce.27.cloned.1.call-start = ((), (), s32[]{:S(2)}) async-start(), calls=%async_computation.10 | async-start | bytes 29245440 | tf_op jit(solution)/shard_map/psum | solution.py:198
  1039.9 7.6 copy-start.58
  1039.9 7.6 copy-start.63
  1039.9 7.6 copy-start.12
  1039.9 7.6 copy-start.14
  1040.0 7.6 copy-start.15
  1040.0 7.6 copy-start.27
  1047.5 10.1 copy-start.32
  1047.6 10.1 copy-start.42
  1047.6 10.0 copy-start.56
  1047.6 22.8 %copy-start.45 = (f32[256]{0:T(256)S(1)}, f32[256]{0:T(256)}, u32[]{:S(2)}) copy-start(f32[256]{0:T(256)} %copy-done.44) | copy-start | bytes 3076
  1047.6 22.8 %copy-start.13 = (bf16[1,256,1536]{2,1,0:T(8,128)(2,1)S(1)}, bf16[1,256,1536]{2,1,0:T(8,128)(2,1)}, u32[]{:S(2)}) copy-start(bf16[1,256,1536]{2,1,0:T(8,128)(2,1)} %param.16) | copy-start | bytes 2359300
  1047.6 22.8 %copy-start.20 = (bf16[1,256,1536]{2,1,0:T(8,128)(2,1)S(1)}, bf16[1,256,1536]{2,1,0:T(8,128)(2,1)}, u32[]{:S(2)}) copy-start(bf16[1,256,1536]{2,1,0:T(8,128)(2,1)} %param.27) | copy-start | bytes 2359300
  1527.4 8.5 copy-start.18
  (27 other events, 66.6 us)
Sparse Core Ops, SparseCore 0:
  9.7 127.6 all-gather.9
  174.6 174.9 all-gather.13
  351.2 62.4 all-gather.11
  441.0 176.4 all-gather.15
  619.9 137.6 reduce-scatter.7
  760.3 276.4 reduce-scatter.5
  1039.9 29.6 reduce-scatter.9
  1074.5 452.8 all-reduce.26
where the time goes:
time: 1550 us
  waiting for transfers between devices  1090 us (70%)
  matrix products  135 us (9%)
  other arithmetic  113 us (7%)
  blocking collectives  95.4 us (6%)
  local copies, waits for them, and re-layouts  88.4 us (6%)
  between operations  20.1 us (1%)
    psum x1, waiting for transfers between devices, per_device(): lax.psum((shares[0], shares[1], shares[2], shares[3], shares[4], shares[5...  415 us
    reduce_scatter x1, waiting for transfers between devices, per_device(): lax.psum_scatter(grad_in_w, 'fsdp', scatter_dimension=0, tiled=True)  279 us
    all_gather x2, waiting for transfers between devices, carried_in(): everything = jax.tree.map(lambda part: lax.all_gather(part, axis), value)  257 us
    all_gather x1, waiting for transfers between devices, per_device(): lax.all_gather(in_weight, 'fsdp', axis=0, tiled=True)  105 us
    select_n x16, other arithmetic, lap(): return jax.tree.map(lambda a, b: jnp.where(reached, a, b), new, before)  56.7 us
    psum x1, blocking collectives, per_device(): lax.psum((shares[0], shares[1], shares[2], shares[3], shares[4], shares[5...  39.6 us
    dot_general x3, matrix products, local_scan(): local_out = jnp.einsum('stuh,suhp->sthp', mixing, values, precision=triple)  35.7 us
  transfers between devices with their start and end apart: 10, of which 8 were waited for; matrix products, arithmetic and copies ran while one was open for 17% of the time, Pallas kernels for 0%

commit v1 on v0

--- a/solution.py
+++ b/solution.py
@@ -5,6 +5,27 @@
 
 epsilon = 1e-05
 triple = lax.Precision.HIGH
+
+
+def ring_gather(x, axis, dim):
+    count, mine, rows = (lax.axis_size(axis), lax.axis_index(axis), x.shape[dim])
+    right = [(i, (i + 1) % count) for i in range(count)]
+    behind = [(i, (i - 1) % count) for i in range(count)]
+    whole = jnp.zeros((*x.shape[:dim], count * rows, *x.shape[dim + 1 :]), x.dtype)
+    whole = lax.dynamic_update_slice_in_dim(whole, x, mine * rows, axis=dim)
+    from_left = from_right = x
+    halfway = count // 2
+    for step in range(1, halfway + 1):
+        from_left = lax.ppermute(from_left, axis, right)
+        whole = lax.dynamic_update_slice_in_dim(
+            whole, from_left, (mine - step) % count * rows, axis=dim
+        )
+        if step < count - halfway:
+            from_right = lax.ppermute(from_right, axis, behind)
+            whole = lax.dynamic_update_slice_in_dim(
+                whole, from_right, (mine + step) % count * rows, axis=dim
+            )
+    return whole
 
 
 def from_behind(value, axis, by):
@@ -90,7 +111,7 @@
 ):
     gathered = (
         lax.all_gather(norm_gain, "fsdp", axis=0, tiled=True),
-        lax.all_gather(in_weight, "fsdp", axis=0, tiled=True),
+        ring_gather(in_weight, "fsdp", 0),
         lax.all_gather(conv_weight, "fsdp", axis=1, tiled=True),
         lax.all_gather(conv_bias, "fsdp", axis=0, tiled=True),
         lax.all_gather(dt_bias, "fsdp", axis=0, tiled=True),

time: 1550 us -> 1770 us (1.14)
  waiting for transfers between devices: 1090 us -> 1200 us
  blocking collectives: 95.4 us -> 146 us
  local copies, waits for them, and re-layouts: 88.4 us -> 118 us
    ppermute x0 -> x3, waiting for transfers between devices: none -> 105 us  [the longest x2 105 us: ring_gather(): from_left = lax.ppermute(from_left, axis, right)]
    all_gather x1, blocking collectives: 6.22 us -> 54.7 us  [per_device(): lax.all_gather(conv_weight, 'fsdp', axis=1, tiled=True)]
    dynamic_update_slice x0 -> x4, local copies, waits for them, and re-layouts: none -> 19 us  [the longest x2 10.6 us: ring_gather(): lax.dynamic_update_slice_in_dim(whole, from_left, (mine - step) % count *...]
  transfers between devices with their start and end apart: 10 -> 13, of which waited for: 8 -> 10; matrix products, arithmetic and copies ran while one was open for 17% -> 17% of each run, Pallas kernels for 0% -> 0%
where the time goes in v1:
time: 1770 us; the launch traced here: 1760 us
  waiting for transfers between devices  1200 us (68%)
  blocking collectives  146 us (8%)
  matrix products  137 us (8%)
  local copies, waits for them, and re-layouts  118 us (7%)
  other arithmetic  115 us (6%)
  starting transfers between devices  20.3 us (1%)
  between operations  20.2 us (1%)
    psum x1, waiting for transfers between devices, per_device(): lax.psum((shares[0], shares[1], shares[2], shares[3], shares[4], shares[5...  418 us
    reduce_scatter x1, waiting for transfers between devices, per_device(): lax.psum_scatter(grad_in_w, 'fsdp', scatter_dimension=0, tiled=True)  279 us
    all_gather x2, waiting for transfers between devices, carried_in(): everything = jax.tree.map(lambda part: lax.all_gather(part, axis), value)  248 us
    all_gather x1, waiting for transfers between devices, per_device(): lax.all_gather(in_weight, 'fsdp', axis=0, tiled=True)  116 us
    ppermute x2, waiting for transfers between devices, ring_gather(): from_left = lax.ppermute(from_left, axis, right)  105 us
    select_n x16, other arithmetic, lap(): return jax.tree.map(lambda a, b: jnp.where(reached, a, b), new, before)  56.9 us
    all_gather x1, blocking collectives, per_device(): lax.all_gather(conv_weight, 'fsdp', axis=1, tiled=True)  54.7 us
    psum x1, blocking collectives, per_device(): lax.psum((shares[0], shares[1], shares[2], shares[3], shares[4], shares[5...  39.2 us
  transfers between devices with their start and end apart: 13, of which 10 were waited for; matrix products, arithmetic and copies ran while one was open for 17% of the time, Pallas kernels for 0%

profile of v1, /device:TPU:0, one launch (start us, length us, event | category | flops | bytes accessed | tf_op | source)
XLA Modules:
  0.0 1757.4 jit_solution(6066765341839422583)
XLA Ops:
  9.7 105.0 %collective-permute-done = bf16[384,6448]{0,1:T(8,128)(2,1)} collective-permute-done((bf16[384,6448]{0,1:T(8,128)(2,1)}, bf16[384,6448]{0,1:T(8,128)(2,1)}, u32[]{:S(2)}, u32[]{:S(2)}) %collective-permute-start) | collective-permute-done | bytes 4952096 | tf_op jit(solution)/shard_map/ppermute | solution.py:19
  117.2 54.7 %all-gather.3 = bf16[4,832,4]{1,2,0:T(4,128)(2,1)S(1)} all-gather(bf16[1,832,4]{1,2,0:T(4,128)(2,1)} %bitcast.345), channel_id=1, replica_groups=mesh['seq'=8,'fsdp'=4] {'fsdp'}, dimensions={0}, use_global_device_ids=true | all-gather | bytes 33280 | tf_op jit(solution)/shard_map/all_gather | solution.py:115
  172.8 8.2 all-gather.2
  187.0 7.6 all-reduce.24
  197.6 7.1 broadcast_in_dim.91
  207.6 5.2 constant_dynamic-update-slice_fusion.2
  212.9 5.5 constant_dynamic-update-slice_fusion.1
  218.3 5.4 constant_dynamic-update-slice_fusion
  223.7 9.9 fusion.6
  247.0 4.2 multiply_convert_fusion
  262.1 5.4 all-gather.4
  279.9 19.3 %all_gather.51 = f32[8,1,48]{2,1,0:T(1,128)} all-gather(f32[1,1,48]{2,1,0:T(1,128)} %get-tuple-element.423), channel_id=1, replica_groups=mesh['seq'=8,'fsdp'=4] {'seq'}, dimensions={0}, use_global_device_ids=true | all-gather | bytes 1728 | tf_op jit(solution)/shard_map/all_gather | solution.py:39
  304.5 131.0 %all-gather.14.cloned.1.call-done = f32[384,64,128]{2,1,0:T(8,128)} async-done(((f32[48,64,128]{2,1,0:T(8,128)}), f32[384,64,128]{2,1,0:T(8,128)}) %all-gather.14.cloned.1.call-update) | async-done | bytes 12582928 | tf_op jit(solution)/shard_map/all_gather | solution.py:39
  435.6 36.0 %while.30 = (s32[]{:T(128)}, f32[1,48,64,128]{3,2,1,0:T(8,128)}, s32[]{:T(128)}, f32[8,1,48]{2,1,0:T(1,128)}, f32[8,1,48,64,128]{4,3,2,1,0:T(8,128)}, /*index=5*/s32[]{:T(128)}, s32[]{:T(128)}) while((s32[]{:T(128)}, f32[1,48,64,128]{3,2,1,0:T(8,128)}, s32[]{:T(128)}, f32[8,1,48]{2,1,0:T(1,128)}, f32[8,1,48,64,128]{4,3,2,1,0:T(8,128)}, ...), condition=%wide.region_4.5_spmd.clone, body=%wide.region_3.4_spmd.clone.sunk | while | flops 1572868 | bytes 4719281 | solution.py:52
  445.5 4.0 fusion.142
  474.6 9.6 fusion.34
  487.7 5.1 multiply_reduce_fusion.7
  493.9 5.6 all-gather.10.cloned.1.call-done
  499.6 10.1 fusion.35
  509.7 5.9 multiply_reduce_fusion.5
  522.8 4.0 fusion.94
  526.9 10.4 reduce-scatter.8.cloned.1.call-start
  537.3 11.6 fusion.76
  552.8 14.9 fusion.8
  569.2 4.2 multiply_reduce_fusion.6
  580.1 5.0 fusion.63
  586.8 116.7 %all-gather.16.cloned.1.call-done = f32[384,64,128]{2,1,0:T(8,128)} async-done(((f32[48,64,128]{2,1,0:T(8,128)}), f32[384,64,128]{2,1,0:T(8,128)}) %all-gather.16.cloned.1.call-update) | async-done | bytes 12582928 | tf_op jit(solution)/shard_map/all_gather | solution.py:39
  703.5 39.0 %while.31 = (s32[]{:T(128)}, f32[1,48,64,128]{3,2,1,0:T(8,128)}, s32[]{:T(128)}, f32[8,1,48]{2,1,0:T(1,128)}, f32[8,1,48,64,128]{4,3,2,1,0:T(8,128)}, /*index=5*/s32[]{:T(128)}, s32[]{:T(128)}, s32[]{:T(128)}, s32[]{:T(128)}) while((s32[]{:T(128)}, f32[1,48,64,128]{3,2,1,0:T(8,128)}, s32[]{:T(128)}, f32[8,1,48]{2,1,0:T(1,128)}, ...), condition=%wide.region_8.9_spmd.clone, body=%wide.region_7.8_spmd.clone.sunk | while | flops 1572872 | bytes 4719343 | solution.py:52
  708.7 4.0 fusion.143
  713.8 4.2 fusion.143
  719.1 4.1 fusion.143
  724.4 4.1 fusion.143
  742.5 5.2 fusion.26
  762.6 11.0 fusion.33
  773.5 3.9 copy.190
  777.4 4.7 fusion.69
  782.1 5.5 multiply_reduce_fusion.4
  798.6 18.5 %fusion.61 = f32[1536,6448]{0,1:T(8,128)} fusion(bf16[256,48]{1,0:T(8,128)(2,1)} %bitcast.338, bf16[256,3328]{1,0:T(8,128)(2,1)} %fusion.42, bf16[256,3072]{1,0:T(8,128)(2,1)} %get-tuple-element.412, bf16[1,256,1536]{2,1,0:T(8,128)(2,1)} %param.16, f32[1536]{0:T(1024)S(1)} %reshape.620, f32[256]{0:T(256)S(1)} %fusion.111), kind=kOutput, calls=%fused_computation.114 | convolution fusion | flops 5082390528 | bytes 43711488 | tf_op jit(solution)/shard_map/sqd,sqp->dp/dot_general | solution.py:200
  819.8 23.8 %reduce-scatter.8.cloned.1.call-done = f32[768,1536]{1,0:T(8,128)} async-done(((f32[3072,1536]{1,0:T(8,128)}), f32[768,1536]{1,0:T(8,128)}) %reduce-scatter.8.cloned.1.call-update) | async-done | bytes 4718608 | tf_op jit(solution)/shard_map/reduce_scatter | solution.py:217
  843.6 279.1 %reduce-scatter.6.cloned.1.call-done = f32[384,6448]{0,1:T(8,128)} async-done(((f32[1536,6448]{0,1:T(8,128)}), f32[384,6448]{0,1:T(8,128)}) %reduce-scatter.6.cloned.1.call-update) | async-done | bytes 9904144 | tf_op jit(solution)/shard_map/reduce_scatter | solution.py:210
  1125.9 7.4 fusion.39
  1133.4 115.7 %all-gather.12.cloned.1.call-done = bf16[1536,6448]{0,1:T(8,128)(2,1)} async-done(((bf16[384,6448]{0,1:T(8,128)(2,1)}), bf16[1536,6448]{0,1:T(8,128)(2,1)}) %all-gather.12.cloned.1.call-update) | async-done | bytes 19808272 | tf_op jit(solution)/shard_map/all_gather | solution.py:167
  1249.1 13.2 fusion.44
  1262.4 11.3 all-reduce.23
  1275.8 5.7 reduce-scatter.10.cloned.1.call-done
  1282.7 39.2 %all-reduce.21 = (f32[384]{0:T(512)}, f32[4,832]{1,0:T(4,128)}, f32[832]{0:T(1024)}, f32[12]{0:T(128)}, f32[12]{0:T(128)}, /*index=5*/f32[12]{0:T(128)}, f32[768]{0:T(1024)}) all-reduce(f32[384]{0:T(512)S(1)} %dynamic-slice.5, f32[4,832]{1,0:T(4,128)S(1)} %copy.211, ...), channel_id=1, replica_groups=mesh['seq'=8,'fsdp'=4] {'seq'}, use_global_device_ids=true, to_apply=%region_21.22 | all-reduce | flops 5348 | bytes 42784 | tf_op jit(solution)/shard_map/psum | solution.py:219
  1321.8 417.6 %all-reduce.27.cloned.1.call-done = (f32[384,6448]{0,1:T(8,128)}, f32[768,1536]{1,0:T(8,128)}) async-done(((f32[384,6448]{0,1:T(8,128)}, f32[768,1536]{1,0:T(8,128)}), (f32[384,6448]{0,1:T(8,128)}, f32[768,1536]{1,0:T(8,128)})) %all-reduce.27.cloned.1.call-update) | async-done | bytes 14622736 | tf_op jit(solution)/shard_map/psum | solution.py:219
  1739.5 8.5 copy.235
  (266 shorter events, 175.0 us)
Async XLA Ops:
  7.2 428.4 %all-gather.14.cloned.1.call-start = ((), (), s32[]{:S(2)}) async-start(), calls=%async_computation.7 | async-start | bytes 14155776 | tf_op jit(solution)/shard_map/all_gather | solution.py:39
  7.2 107.5 %collective-permute-start = (bf16[384,6448]{0,1:T(8,128)(2,1)}, bf16[384,6448]{0,1:T(8,128)(2,1)}, u32[]{:S(2)}, u32[]{:S(2)}) collective-permute-start(bf16[384,6448]{0,1:T(8,128)(2,1)} %param.19), channel_id=1, source_target_pairs={{0,1},{1,2},{2,3},{3,0},{4,5},{5,6},{6,7},{7,4},{8,9},{9,10},{10,1... | collective-permute-start | bytes 14856200 | tf_op jit(solution)/shard_map/ppermute | solution.py:19
  7.7 205.1 %collective-permute-start.1 = (bf16[384,6448]{0,1:T(8,128)(2,1)}, bf16[384,6448]{0,1:T(8,128)(2,1)}, u32[]{:S(2)}, u32[]{:S(2)}) collective-permute-start(bf16[384,6448]{0,1:T(8,128)(2,1)} %param.19), channel_id=1, source_target_pairs={{0,3},{1,0},{2,1},{3,2},{4,7},{5,4},{6,5},{7,6},{8,11},{9,8},{10,9... | collective-permute-start | bytes 14856200 | tf_op jit(solution)/shard_map/ppermute | solution.py:24
  114.7 103.6 %collective-permute-start.2 = (bf16[384,6448]{0,1:T(8,128)(2,1)}, bf16[384,6448]{0,1:T(8,128)(2,1)}, u32[]{:S(2)}, u32[]{:S(2)}) collective-permute-start(bf16[384,6448]{0,1:T(8,128)(2,1)} %collective-permute-done), channel_id=1, source_target_pairs={{0,1},{1,2},{2,3},{3,0},{4,5},{5,6},{6,7},{7,4},{8,9},{9,10},{10,1... | collective-permute-start | bytes 14856200 | tf_op jit(solution)/shard_map/ppermute | solution.py:19
  194.7 10.0 copy-start.52
  195.3 47.1 %copy-start.37 = (f32[48]{0:T(128)}, f32[48]{0:T(128)S(1)}, u32[]{:S(2)}) copy-start(f32[48]{0:T(128)S(1)} %convert_element_type.95) | copy-start | bytes 580
  196.0 8.6 slice-start
  197.5 7.1 copy-start.41
  197.6 36.1 %copy-start.49 = (f32[48]{0:T(128)}, f32[48]{0:T(128)S(1)}, u32[]{:S(2)}) copy-start(f32[48]{0:T(128)S(1)} %convert_exponential_fusion) | copy-start | bytes 580
  197.6 7.1 slice-start.1
  218.3 5.4 copy-start.11
  233.6 11.5 copy-start.10
  237.8 7.4 collective-permute-start.3
  256.5 5.7 copy-start.48
  260.1 239.4 %all-gather.10.cloned.1.call-start = ((), (), s32[]{:S(2)}) async-start(), calls=%async_computation.3 | async-start | bytes 11796480 | tf_op jit(solution)/shard_map/all_gather | solution.py:121
  260.9 442.6 %all-gather.16.cloned.1.call-start = ((), (), s32[]{:S(2)}) async-start(), calls=%async_computation.8 | async-start | bytes 14155776 | tf_op jit(solution)/shard_map/all_gather | solution.py:39
  474.2 10.0 copy-start.8
  499.6 10.1 copy-start.44
  499.6 10.1 copy-start
  499.6 10.1 copy-start.3
  499.6 10.1 copy-start.6
  499.6 10.1 copy-start.35
  509.7 7.6 copy-start.9
  526.9 316.7 %reduce-scatter.8.cloned.1.call-start = ((), (), s32[]{:S(2)}) async-start(), calls=%async_computation.6 | async-start | bytes 23592960 | tf_op jit(solution)/shard_map/reduce_scatter | solution.py:217
  549.0 573.7 %reduce-scatter.6.cloned.1.call-start = ((), (), s32[]{:S(2)}) async-start(), calls=%async_computation.5 | async-start | bytes 49520640 | tf_op jit(solution)/shard_map/reduce_scatter | solution.py:210
  578.1 7.0 copy-start.19
  749.2 3.6 copy-start.21
  749.2 3.6 copy-start.22
  777.4 4.7 copy-start.7
  782.1 5.5 copy-start.26
  782.1 5.5 copy-start.27
  782.1 5.5 copy-start.28
  788.6 4.5 copy-start.38
  788.7 4.5 copy-start.46
  790.3 6.0 collective-permute-start.4
  817.2 431.9 %all-gather.12.cloned.1.call-start = ((), (), s32[]{:S(2)}) async-start(), calls=%async_computation.4 | async-start | bytes 24760320 | tf_op jit(solution)/shard_map/all_gather | solution.py:167
  817.7 463.8 %reduce-scatter.10.cloned.1.call-start = ((), (), s32[]{:S(2)}) async-start(), calls=%async_computation.9 | async-start | bytes 2129920
  819.8 919.7 %all-reduce.27.cloned.1.call-start = ((), (), s32[]{:S(2)}) async-start(), calls=%async_computation.10 | async-start | bytes 29245440 | tf_op jit(solution)/shard_map/psum | solution.py:219
  1125.9 7.4 copy-start.51
  1125.9 7.4 copy-start.53
  1125.9 123.2 %copy-start.24 = (bf16[1,256,48]{2,1,0:T(8,128)(2,1)S(1)}, bf16[1,256,48]{2,1,0:T(8,128)(2,1)}, u32[]{:S(2)}) copy-start(bf16[1,256,48]{2,1,0:T(8,128)(2,1)} %get-tuple-element.404) | copy-start | bytes 73732
  1133.3 129.0 %copy-start.29 = (f32[3328]{0:T(1024)S(1)}, f32[3328]{0:T(1024)}, u32[]{:S(2)}) copy-start(f32[3328]{0:T(1024)} %get-tuple-element.355) | copy-start | bytes 39940
  1133.3 129.0 %copy-start.39 = (f32[3072]{0:T(1024)S(1)}, f32[3072]{0:T(1024)}, u32[]{:S(2)}) copy-start(f32[3072]{0:T(1024)} %get-tuple-element.353) | copy-start | bytes 36868
  1133.3 129.0 %copy-start.50 = (f32[48]{0:T(128)S(1)}, f32[48]{0:T(128)}, u32[]{:S(2)}) copy-start(f32[48]{0:T(128)} %get-tuple-element.403) | copy-start | bytes 580
  1133.4 140.7 %copy-start.42 = (f32[256]{0:T(256)S(1)}, f32[256]{0:T(256)}, u32[]{:S(2)}) copy-start(f32[256]{0:T(256)} %copy-done.41) | copy-start | bytes 3076
  1133.4 140.7 %copy-start.12 = (bf16[1,256,1536]{2,1,0:T(8,128)(2,1)S(1)}, bf16[1,256,1536]{2,1,0:T(8,128)(2,1)}, u32[]{:S(2)}) copy-start(bf16[1,256,1536]{2,1,0:T(8,128)(2,1)} %param.16) | copy-start | bytes 2359300
  1133.4 140.7 %copy-start.17 = (bf16[1,256,1536]{2,1,0:T(8,128)(2,1)S(1)}, bf16[1,256,1536]{2,1,0:T(8,128)(2,1)}, u32[]{:S(2)}) copy-start(bf16[1,256,1536]{2,1,0:T(8,128)(2,1)} %param.27) | copy-start | bytes 2359300
  1739.5 8.5 copy-start.15
  (22 other events, 49.6 us)
Sparse Core Ops, SparseCore 0:
  260.3 175.2 all-gather.13
  437.1 62.4 all-gather.9
  527.0 176.4 all-gather.15
  705.9 137.6 reduce-scatter.7
  846.3 276.4 reduce-scatter.5
  1124.2 124.8 all-gather.11
  1252.2 29.2 reduce-scatter.9
  1286.4 453.0 all-reduce.26
